TPU v7x, 32 devices: a whole 2x2x4 slice. The times are simulated.
32 devices in a mesh: dp: 16 (over z, x, core), tensor: 2 (over y).
Axes of the slice: x: 2, y: 2, z: 4, core: 2. Of those that a mesh axis runs over, the one named last changes fastest.
Arguments:
- x_in: bfloat16 [16384, 2048], P('dp'), may hold values from -6 to 6
- norm_gain: float32 [2048], replicated, may hold values from 0.5 to 1.5
- w_zx: bfloat16 [2048, 2, 4096], P(None, None, 'tensor'), may hold values from -0.125 to 0.125
- w_bc: bfloat16 [2048, 256], replicated, may hold values from -0.125 to 0.125
- w_dt: bfloat16 [2048, 64], P(None, 'tensor'), may hold values from -0.125 to 0.125
- conv_x: float32 [5, 4096], P(None, 'tensor'), may hold values from -3 to 3
- conv_bc: float32 [5, 256], replicated, may hold values from -3 to 3
- dt_bias: float32 [64], P('tensor'), may hold values from -4 to -1
- a_log: float32 [64], P('tensor'), may hold values from -3 to 1.5
- d_skip: float32 [64], P('tensor'), may hold values from 0.5 to 1.5
- gate_gain: float32 [4096], P('tensor'), may hold values from 0.5 to 1.5
- w_out: bfloat16 [4096, 2048], P('tensor'), may hold values from -0.09375 to 0.09375
- cotangent: bfloat16 [16384, 2048], P('dp'), may hold values from -6 to 6
- block_parent: int32 [128], P('dp'), may hold values from -1 to 6, as said below
Outputs:
- mixed: bfloat16 [16384, 2048], P('dp')
- input_grad: bfloat16 [16384, 2048], P('dp')
- norm_gain_grad: float32 [2048], replicated
- w_zx_grad: float32 [2048, 2, 4096], P('dp', None, 'tensor')
- w_bc_grad: float32 [2048, 256], replicated
- w_dt_grad: float32 [2048, 64], P('dp', 'tensor')
- conv_x_grad: float32 [5, 4096], P(None, 'tensor')
- conv_bc_grad: float32 [5, 256], replicated
- dt_bias_grad: float32 [64], P('tensor')
- a_log_grad: float32 [64], P('tensor')
- d_skip_grad: float32 [64], P('tensor')
- gate_gain_grad: float32 [4096], P('tensor')
- w_out_grad: float32 [4096, 2048], P('tensor', 'dp')
Inputs may be any that keep to these rules, and one draw needn't show every extreme that they name: `block_parent`: each device's 8 blocks hold one tree. A block's entry is the index, among its device's blocks, of an earlier block whose last token precedes its first token, or -1 at the root; the first half of the blocks or more form a chain from the root, and the last block continues the block before it.
All inputs are finite; a program needn't handle non-finite values.
Results may differ from a plain program's by a relative error of at most 0.014.
Values may be sent and summed in bfloat16 or wider, within the bound.
No kernel may reach another device: no remote copies, remote signals or barrier semaphores. Data moves between devices by JAX's collectives and lax.ppermute only.
A program may use at most 320 MiB of HBM per device.

v0:
```python
import jax
import jax.numpy as jnp
from jax import lax
from jax.sharding import PartitionSpec as P

epsilon = 1e-05
highest = lax.Precision.HIGHEST


def conv_path(inputs, kernel, parent):
    blocks = parent.shape[0]
    tokens, channels = inputs.shape
    window = kernel.shape[0] - 1
    block_len = tokens // blocks
    blocked = inputs.reshape(blocks, block_len, channels)
    trailing = blocked[:, block_len - (window - 1) :, :]
    context = jnp.take(trailing, jnp.maximum(parent, 0), axis=0)
    context = jnp.where((parent >= 0)[:, None, None], context, jnp.zeros_like(context))
    padded = jnp.concatenate([context, blocked], axis=1)
    summed = kernel[window][None, None, :] + jnp.zeros_like(blocked)
    for offset in range(window):
        summed = summed + kernel[offset][None, None, :] * padded[:, offset : offset + block_len, :]
    return jax.nn.silu(summed).reshape(tokens, channels)


def decay_paths(block_decay, parent):
    blocks = parent.shape[0]
    n_heads = block_decay.shape[1]
    parent_map = (parent[:, None] == jnp.arange(blocks, dtype=jnp.int32)[None, :]).astype(
        jnp.float32
    )
    identity = jnp.eye(blocks, dtype=jnp.float32)

    def advance(turn, paths):
        return identity[None] + jnp.einsum(
            "hb,bp,hpa->hba", block_decay.T, parent_map, paths, precision=highest
        )

    paths = lax.fori_loop(0, blocks, advance, jnp.broadcast_to(identity, (n_heads, blocks, blocks)))
    return (paths, parent_map)


def ssd_mix(x_heads, b_rows, c_rows, dt_raw, dt_bias, a_log, d_skip, parent):
    tokens, n_heads, head_dim = x_heads.shape
    blocks = parent.shape[0]
    block_len = tokens // blocks
    dt_values = jax.nn.softplus(dt_raw + dt_bias)
    log_rate = dt_values * -jnp.exp(a_log)
    x_blocks = x_heads.reshape(blocks, block_len, n_heads, head_dim)
    b_blocks = b_rows.reshape(blocks, block_len, -1)
    c_blocks = c_rows.reshape(blocks, block_len, -1)
    dt_blocks = dt_values.reshape(blocks, block_len, n_heads)
    cumulant = jnp.cumsum(log_rate.reshape(blocks, block_len, n_heads), axis=1)
    scores = jnp.einsum("bin,bjn->bij", c_blocks, b_blocks, precision=highest)
    rows_idx = jnp.arange(block_len, dtype=jnp.int32)
    causal = (rows_idx[:, None] >= rows_idx[None, :])[None, :, :, None]
    log_gap = cumulant[:, :, None, :] - cumulant[:, None, :, :]
    decays = jnp.where(causal, jnp.exp(jnp.where(causal, log_gap, 0.0)), 0.0)
    weights = scores[..., None] * decays * dt_blocks[:, None, :, :]
    within = jnp.einsum("bijh,bjhp->bihp", weights, x_blocks, precision=highest)
    to_end = jnp.exp(cumulant[:, -1:, :] - cumulant) * dt_blocks
    local_states = jnp.einsum("bjh,bjhp,bjn->bhpn", to_end, x_blocks, b_blocks, precision=highest)
    paths, parent_map = decay_paths(jnp.exp(cumulant[:, -1, :]), parent)
    end_states = jnp.einsum("hba,ahpn->bhpn", paths, local_states, precision=highest)
    start_states = jnp.einsum("bq,qhpn->bhpn", parent_map, end_states, precision=highest)
    carried = jnp.exp(cumulant)[..., None] * jnp.einsum(
        "bin,bhpn->bihp", c_blocks, start_states, precision=highest
    )
    result = within + carried + d_skip[None, None, :, None] * x_blocks
    return result.reshape(tokens, n_heads * head_dim)


def gated_mix(x_heads, bc_rows, dt_raw, dt_bias, a_log, d_skip, z_gate, parent):
    half = bc_rows.shape[1] // 2
    mixed_heads = ssd_mix(
        x_heads, bc_rows[:, :half], bc_rows[:, half:], dt_raw, dt_bias, a_log, d_skip, parent
    )
    return mixed_heads * jax.nn.silu(z_gate)


def over_tokens(left, right):
    return lax.dot_general(
        left, right, (((0,), (0,)), ((), ())), preferred_element_type=jnp.float32
    )


def over_columns(left, right):
    return lax.dot_general(
        left, right, (((1,), (1,)), ((), ())), preferred_element_type=jnp.float32
    )


def rounded(value):
    return lax.optimization_barrier(value.astype(jnp.bfloat16)).astype(jnp.float32)


def local(
    x_in,
    norm_gain,
    w_zx,
    w_bc,
    w_dt,
    conv_x,
    conv_bc,
    dt_bias,
    a_log,
    d_skip,
    gate_gain,
    w_out,
    cotangent,
    block_parent,
):
    tokens, features = x_in.shape
    local_heads = w_dt.shape[1]
    inner_width = w_zx.shape[2]
    head_dim = inner_width // local_heads
    full_width = inner_width * lax.axis_size("tensor")
    x_float = x_in.astype(jnp.float32)
    inv_rms = lax.rsqrt(jnp.mean(x_float * x_float, axis=-1) + epsilon)
    normed = (x_float * inv_rms[:, None] * norm_gain).astype(jnp.bfloat16)
    z_gate = jnp.dot(normed, w_zx[:, 0, :], preferred_element_type=jnp.float32)
    x_pre = jnp.dot(normed, w_zx[:, 1, :], preferred_element_type=jnp.float32)
    bc_pre = jnp.dot(normed, w_bc, preferred_element_type=jnp.float32)
    dt_raw = jnp.dot(normed, w_dt, preferred_element_type=jnp.float32)

    def x_piece(values, kernel):
        return conv_path(values, kernel, block_parent)

    x_conv, x_pull = jax.vjp(x_piece, x_pre, conv_x)
    bc_conv, bc_pull = jax.vjp(x_piece, bc_pre, conv_bc)
    x_round = rounded(x_conv)
    bc_round = rounded(bc_conv)

    def mixer(x_values, bc_values, dt_values, bias_values, log_values, skip_values, gate_values):
        return gated_mix(
            x_values.reshape(tokens, local_heads, head_dim),
            bc_values,
            dt_values,
            bias_values,
            log_values,
            skip_values,
            gate_values,
            block_parent,
        )

    gated, mix_pull = jax.vjp(mixer, x_round, bc_round, dt_raw, dt_bias, a_log, d_skip, z_gate)
    squares = lax.psum(jnp.sum(gated * gated, axis=-1), "tensor")
    inv_gate = lax.rsqrt(squares / full_width + epsilon)
    gate_normed = (gated * inv_gate[:, None] * gate_gain).astype(jnp.bfloat16)
    partial_out = jnp.dot(gate_normed, w_out, preferred_element_type=jnp.float32)
    share = tokens // lax.axis_size("tensor")
    first_row = lax.axis_index("tensor") * share
    x_rows = lax.dynamic_slice_in_dim(x_float, first_row, share, 0)
    mixed = (
        x_float + lax.psum(partial_out.astype(jnp.bfloat16), "tensor").astype(jnp.float32)
    ).astype(jnp.bfloat16)
    d_gate_normed = over_columns(cotangent, w_out)
    w_out_part = over_tokens(gate_normed, cotangent)
    gate_gain_part = jnp.sum(d_gate_normed * gated * inv_gate[:, None], axis=0)
    scaled = d_gate_normed * gate_gain
    cross = lax.psum(jnp.sum(scaled * gated, axis=-1), "tensor")
    d_gated = (
        inv_gate[:, None] * scaled
        - gated * (inv_gate * inv_gate * inv_gate * cross / full_width)[:, None]
    )
    d_x_round, d_bc_round, d_dt_raw, dt_bias_part, a_log_part, d_skip_part, d_z_gate = mix_pull(
        d_gated
    )
    d_x_pre, conv_x_part = x_pull(d_x_round)
    d_bc_pre, conv_bc_part = bc_pull(d_bc_round)
    z_low = d_z_gate.astype(jnp.bfloat16)
    x_low = d_x_pre.astype(jnp.bfloat16)
    bc_low = d_bc_pre.astype(jnp.bfloat16)
    dt_low = d_dt_raw.astype(jnp.bfloat16)
    w_zx_part = jnp.stack([over_tokens(normed, z_low), over_tokens(normed, x_low)], axis=1)
    w_bc_part = over_tokens(normed, bc_low)
    w_dt_part = over_tokens(normed, dt_low)
    d_normed = over_columns(z_low, w_zx[:, 0, :]) + over_columns(x_low, w_zx[:, 1, :])
    d_normed = d_normed + over_columns(bc_low, w_bc) + over_columns(dt_low, w_dt)
    norm_gain_part = jnp.sum(d_normed * x_float * inv_rms[:, None], axis=0)
    d_rows = lax.psum_scatter(
        d_normed.astype(jnp.bfloat16), "tensor", scatter_dimension=0, tiled=True
    ).astype(jnp.float32)
    rms_rows = lax.dynamic_slice_in_dim(inv_rms, first_row, share, 0)
    cot_rows = lax.dynamic_slice_in_dim(cotangent, first_row, share, 0).astype(jnp.float32)
    gained = d_rows * norm_gain
    spread = rms_rows * rms_rows * rms_rows * jnp.sum(gained * x_rows, axis=-1) / features
    d_input = cot_rows + rms_rows[:, None] * gained - x_rows * spread[:, None]
    input_grad = lax.all_gather(d_input.astype(jnp.bfloat16), "tensor", axis=0, tiled=True)
    w_zx_grad, w_dt_grad, w_out_grad = (
        lax.psum_scatter(
            w_zx_part.astype(jnp.bfloat16), "dp", scatter_dimension=0, tiled=True
        ).astype(jnp.float32),
        lax.psum_scatter(
            w_dt_part.astype(jnp.bfloat16), "dp", scatter_dimension=0, tiled=True
        ).astype(jnp.float32),
        lax.psum_scatter(
            w_out_part.astype(jnp.bfloat16), "dp", scatter_dimension=1, tiled=True
        ).astype(jnp.float32),
    )
    conv_x_grad, dt_bias_grad, a_log_grad, d_skip_grad, gate_gain_grad = lax.psum(
        (conv_x_part, dt_bias_part, a_log_part, d_skip_part, gate_gain_part), "dp"
    )
    norm_gain_grad, w_bc_grad, conv_bc_grad = lax.psum(
        (norm_gain_part, w_bc_part, conv_bc_part), ("dp", "tensor")
    )
    return (
        mixed,
        input_grad,
        norm_gain_grad,
        w_zx_grad,
        w_bc_grad,
        w_dt_grad,
        conv_x_grad,
        conv_bc_grad,
        dt_bias_grad,
        a_log_grad,
        d_skip_grad,
        gate_gain_grad,
        w_out_grad,
    )


def solution(mesh):
    return jax.shard_map(
        local,
        mesh=mesh,
        in_specs=(
            P("dp", None),
            P(),
            P(None, None, "tensor"),
            P(),
            P(None, "tensor"),
            P(None, "tensor"),
            P(),
            P("tensor"),
            P("tensor"),
            P("tensor"),
            P("tensor"),
            P("tensor", None),
            P("dp", None),
            P("dp"),
        ),
        out_specs=(
            P("dp", None),
            P("dp", None),
            P(),
            P("dp", None, "tensor"),
            P(),
            P("dp", "tensor"),
            P(None, "tensor"),
            P(),
            P("tensor"),
            P("tensor"),
            P("tensor"),
            P("tensor"),
            P("tensor", "dp"),
        ),
        check_vma=False,
    )
```

profile of v0, /device:TPU:0, one launch (start us, length us, event | category | flops | bytes accessed | tf_op | source)
XLA Modules:
  0.0 1176.5 jit_solution(15319442505596880165)
XLA Ops:
  12.6 32.8 %fusion.165 = (bf16[2048,1,2048]{2,1,0:T(2,128)(2,1)}, bf16[2048,1,2048]{2,1,0:T(2,128)(2,1)}) fusion(bf16[2048,2,2048]{2,1,0:T(2,128)(2,1)} %param.20), kind=kLoop, calls=%fused_computation.254 | loop fusion | bytes 33554432 | tf_op jit(solution)/shard_map/slice | solution.py:121
  64.3 16.3 %multiply_convert_fusion.1 = (bf16[8,128,2048]{2,1,0:T(8,128)(2,1)}, f32[8,128,2048]{2,1,0:T(8,128)}) fusion(f32[8,128,2048]{2,1,0:T(8,128)} %copy-done.7, f32[2048]{0:T(1024)S(1)} %bitcast.305, f32[8,3,2048]{2,1,0:T(4,128)S(1)} %select_select_fusion, f32[2048]{0:T(1024)S(1)} %bitcast.307, f32[2048]{0:T(1024)S(1)} %bitcast.301, f32[2048]{0:T(1024)S(1)} %bitcast.303, ...), kind=kLoop, calls=%fused_computation.101 | loop fusion | flops 33554432 | bytes 21209088 | tf_op jit(solution)/shard_map/convert_element_type | solution.py:94
  104.8 23.3 %fusion.171 = f32[8,128,32]{2,0,1:T(8,128)S(1)} fusion(f32[8,128,32]{2,0,1:T(8,128)S(1)} %copy.143), kind=kOutput, calls=%fused_computation.260 | output fusion | flops 4161536 | bytes 262144 | tf_op jit(solution)/shard_map/jvp(jit(cumsum))/reduce_window_sum | solution.py:53
  211.3 21.9 %fusion.39 = f32[8,128,32,64]{1,3,2,0:T(8,128)} fusion(f32[8,128,32,64]{1,3,2,0:T(8,128)} %copy.158, f32[8,128,32,64]{1,3,2,0:T(8,128)S(1)} %fusion.69, f32[32]{0:T(128)S(1)} %copy-done.90, f32[8,128,32]{1,2,0:T(8,128)S(1)} %copy.148, f32[8,128,32]{1,2,0:T(8,128)S(1)} %bitcast.298, f32[8,128,32]{1,2,0:T(8,128)S(1)} %copy-done.36, ...), kind=kOutput, calls=%fused_computation.62 | convolution fusion | flops 3250585600 | bytes 30294144 | tf_op jit(solution)/shard_map/jvp(bijh,bjhp->bihp)/dot_general | solution.py:60
  233.2 16.2 %copy.215 = f32[8,128,32,64]{3,2,1,0:T(8,128)} copy(f32[8,128,32,64]{1,3,2,0:T(8,128)} %fusion.39) | data formatting | bytes 16777216 | tf_op jit(solution)/shard_map/jvp()/reshape | solution.py:70
  264.3 19.7 %multiply_reduce_fusion.11 = (f32[1024]{0:T(1024)S(1)}, f32[1024,2048]{1,0:T(8,128)}, f32[1024,2048]{1,0:T(8,128)}) fusion(f32[1024,2048]{1,0:T(8,128)} %reshape.284, bf16[1024,2048]{1,0:T(8,128)(2,1)} %copy-done.2, bf16[2048,1,2048]{2,1,0:T(2,128)(2,1)} %get-tuple-element.379), kind=kOutput, calls=%fused_computation.85 | convolution fusion | flops 8604613632 | bytes 37752832 | tf_op jit(solution)/shard_map/dot_general | solution.py:121
  289.9 15.3 %convolution_convert_fusion.1 = bf16[1024,2048]{1,0:T(8,128)(2,1)} fusion(bf16[2048,2048]{1,0:T(8,128)(2,1)} %param.29, f32[1024,2048]{1,0:T(8,128)} %get-tuple-element.373, f32[2048]{0:T(1024)S(1)} %copy-done.73, f32[1024]{0:T(1024)S(1)} %add_rsqrt_fusion), kind=kOutput, calls=%fused_computation.140 | convolution fusion | flops 8598323200 | bytes 20983808 | tf_op jit(solution)/shard_map/dot_general | solution.py:150
  305.2 17.0 %multiply_reduce_fusion.2 = (f32[2048]{0:T(1024)}, f32[1024]{0:T(1024)S(1)}, f32[1024,2048]{1,0:T(8,128)}) fusion(f32[1024,2048]{1,0:T(8,128)} %get-tuple-element.373, f32[1024]{0:T(1024)S(1)} %add_rsqrt_fusion, f32[2048]{0:T(1024)S(1)} %copy-done.73, bf16[1024,2048]{1,0:T(8,128)(2,1)} %param.30, bf16[2048,2048]{1,0:T(8,128)(2,1)} %param.29), kind=kOutput, calls=%fused_computation.70 | convolution fusion | flops 8602514432 | bytes 29384704 | tf_op jit(solution)/shard_map/dot_general | solution.py:88
  327.2 20.5 %multiply_reduce_fusion.3 = (f32[2048]{0:T(1024)}, f32[1024,2048]{1,0:T(8,128)}, bf16[1024,2048]{1,0:T(8,128)(2,1)}) fusion(bf16[1024,2048]{1,0:T(8,128)(2,1)} %bitcast.262, f32[1024,2048]{1,0:T(8,128)} %get-tuple-element.413, f32[1024,2048]{1,0:T(8,128)} %get-tuple-element.373, f32[1024]{0:T(1024)S(1)} %fusion.141, f32[1024,2048]{1,0:T(8,128)} %get-tuple-element.414, ...), kind=kLoop, calls=%fused_computation.71 | loop fusion | flops 41940992 | bytes 50356224 | tf_op jit(solution)/shard_map/transpose(jvp())/reduce_sum | solution.py:69
  391.1 21.3 %fusion.106 = f32[32,8,8]{2,1,0:T(8,128)S(1)} fusion(f32[32,64,128,8]{2,3,1,0:T(8,128)S(1)} %fusion.44, f32[8,32,64,128]{3,2,1,0:T(8,128)S(1)} %bitcast.259), kind=kOutput, calls=%fused_computation.159 | convolution fusion | flops 201326592 | bytes 16785408 | tf_op jit(solution)/shard_map/transpose(jvp(hba,ahpn->bhpn))/dot_general | solution.py:64
  429.7 18.2 %fusion.103 = f32[8,128,128]{2,1,0:T(8,128)S(1)} fusion(f32[8,32,64,128]{3,0,2,1:T(8,128)} %convolution_bitcast_fusion.1, f32[8,128,32]{1,2,0:T(8,128)S(1)} %copy-done.29, bf16[8,128,32,64]{1,0,3,2:T(8,128)(2,1)S(1)} %bitcast.266), kind=kOutput, calls=%fused_computation.156 | convolution fusion | flops 3225419776 | bytes 13238272 | tf_op jit(solution)/shard_map/transpose(jvp(bjh,bjhp,bjn->bhpn))/dot_general | solution.py:62
  448.0 15.7 %fusion.98 = f32[8,128,128]{2,1,0:T(8,128)S(1)} fusion(f32[8,32,64,128]{3,0,2,1:T(8,128)S(1)} %bitcast.257, f32[8,128,32,64]{1,0,3,2:T(8,128)S(1)} %bitcast.252, f32[8,128,32]{1,2,0:T(8,128)S(1)} %copy.148), kind=kOutput, calls=%fused_computation.155 | convolution fusion | flops 3223322624 | bytes 17432576 | tf_op jit(solution)/shard_map/transpose(jvp(bin,bhpn->bihp))/dot_general | solution.py:66
  463.8 28.9 %fusion.28 = (f32[8,128,32]{1,2,0:T(8,128)}, f32[8,128,32]{1,2,0:T(8,128)S(1)}, f32[8,128,32]{1,2,0:T(8,128)}, f32[8,128,128]{2,1,0:T(8,128)S(1)}) fusion(f32[8,128,32]{1,2,0:T(8,128)S(1)} %bitcast.299, f32[8,128,32]{1,2,0:T(8,128)S(1)} %copy-done.37, f32[8,128,128]{2,1,0:T(8,128)S(1)} %copy-done.31, pred[128,128]{1,0:T(8,128)(4,1)S(1)} %copy-done.64, ...), kind=kOutput, calls=%fused_computation.44 | convolution fusion | flops 3283910656 | bytes 14303232 | tf_op jit(solution)/shard_map/transpose(jvp(bijh,bjhp->bihp))/dot_general | solution.py:60
  508.4 23.6 %bitcast_add_fusion = f32[8,128,32,64]{1,3,2,0:T(8,128)} fusion(f32[8,128,32,64]{1,3,2,0:T(8,128)} %fusion.65, f32[8,128,32,64]{1,0,3,2:T(8,128)S(1)} %bitcast.255, f32[32]{0:T(128)S(1)} %copy-done.91, f32[8,128,32]{1,2,0:T(8,128)S(1)} %copy-done.29, f32[8,128,32]{1,2,0:T(8,128)S(1)} %bitcast.300, f32[8,128,32]{1,2,0:T(8,128)S(1)} %copy-done.37, ...), kind=kOutput, calls=%fused_computation.58 | convolution fusion | flops 3250585600 | bytes 34488448 | tf_op jit(solution)/shard_map/transpose(jvp(bijh,bjhp->bihp))/dot_general | solution.py:60
  536.4 36.3 %while.31 = (s32[]{:T(128)}, f32[8,32]{1,0:T(8,128)}, f32[32,8,8]{2,1,0:T(8,128)S(1)}, f32[8,32,8,8]{3,2,1,0:T(8,128)}, s32[8]{0:T(128)}, /*index=5*/f32[8,32]{0...) while((s32[]{:T(128)}, f32[8,32]{1,0:T(8,128)}, f32[32,8,8]{2,1,0:T(8,128)S(1)}, ...), condition=%wide.region_15.16_spmd.clone, body=%wide.region_14.15_spmd.clone.sunk | while | flops 420484 | bytes 210855 | solution.py:39
  590.6 18.6 %multiply_reduce_fusion.6 = (f32[2048]{0:T(1024)}, f32[2048]{0:T(1024)}, f32[2048]{0:T(1024)}, f32[2048]{0:T(1024)}, f32[2048]{0:T(1024)}, /*index=5*/f32[8,128,2048]{2,1,0:T(8,128)S(1)}) fusion(f32[8,128,2048]{2,1,0:T(8,128)} %copy-done.7, f32[8,3,2048]{2,1,0:T(4,128)S(1)} %copy-done.19, f32[8,128,2048]{2,1,0:T(8,128)} %get-tuple-element.377, ...), kind=kLoop, calls=%fused_computation.74 | loop fusion | flops 44029952 | bytes 33792000 | tf_op jit(solution)/shard_map/transpose(jvp())/reduce_sum | solution.py:22
  650.6 15.6 %fusion.87 = f32[1024,2048]{1,0:T(8,128)} fusion(bf16[1024,2048]{1,0:T(8,128)(2,1)S(1)} %copy-done.15, bf16[2048,1,2048]{2,1,0:T(2,128)(2,1)} %get-tuple-element.379), kind=kOutput, calls=%fused_computation.142 | convolution fusion | flops 8589934592 | bytes 20971520 | tf_op jit(solution)/shard_map/dot_general | solution.py:88
  666.2 24.1 %multiply_reduce_fusion.8 = (f32[2048]{0:T(1024)S(1)}, bf16[1024,2048]{1,0:T(8,128)(2,1)}, bf16[1024,2048]{1,0:T(8,128)(2,1)}) fusion(bf16[1024,2048]{1,0:T(8,128)(2,1)} %param.18, f32[1024]{0:T(1024)S(1)} %copy-done.59, bf16[1024,2048]{1,0:T(8,128)(2,1)} %all-reduce.29.cloned.1.call-done, f32[1024,2048]{1,0:T(8,128)} %fusion.138, ...), kind=kOutput, calls=%fused_computation.78 | convolution fusion | flops 8613001216 | bytes 54538240 | tf_op jit(solution)/shard_map/dot_general | solution.py:88
  728.9 17.5 %reduce-scatter.9.cloned.1.call-done = bf16[512,2048]{1,0:T(8,128)(2,1)} async-done(((bf16[1024,2048]{1,0:T(8,128)(2,1)}), bf16[512,2048]{1,0:T(8,128)(2,1)}) %reduce-scatter.9.cloned.1.call-update) | async-done | bytes 2097168 | tf_op jit(solution)/shard_map/reduce_scatter | solution.py:181
  790.7 63.7 %all-reduce.25 = (f32[5,2048]{1,0:T(8,128)}, f32[32]{0:T(128)}, f32[32]{0:T(128)}, f32[32]{0:T(128)}, f32[2048]{0:T(1024)}) all-reduce(f32[5,2048]{1,0:T(8,128)S(1)} %pad_add_fusion.3, f32[32]{0:T(128)S(1)} %get-tuple-element.364, f32[32]{0:T(128)S(1)} %negate_multiply_fusion, ...), channel_id=1, replica_groups=mesh['dp'=16,'tensor'=2] {'dp'}, use_global_device_ids=true, to_apply=%region_32.33 | all-reduce | flops 12384 | bytes 99072 | tf_op jit(solution)/shard_map/psum | solution.py:201
  855.9 39.0 %all-reduce.24 = (f32[2048]{0:T(1024)}, f32[5,256]{1,0:T(8,128)}) all-reduce(f32[2048]{0:T(1024)S(1)} %get-tuple-element.381, f32[5,256]{1,0:T(8,128)S(1)} %pad_add_fusion.4), channel_id=1, replica_groups=mesh['dp'=16,'tensor'=2] {'dp','tensor'}, use_global_device_ids=true, to_apply=%region_23.24 | all-reduce | flops 3328 | bytes 26624 | tf_op jit(solution)/shard_map/psum | solution.py:204
  894.8 22.0 %reduce-scatter.15.cloned.1.call-done = bf16[128,2048]{1,0:T(8,128)(2,1)} async-done(((bf16[2048,2048]{1,0:T(8,128)(2,1)}), bf16[128,2048]{1,0:T(8,128)(2,1)}) %reduce-scatter.15.cloned.1.call-update) | async-done | bytes 524304
  919.2 56.4 %all-gather.2.cloned.1.call-done = bf16[1024,2048]{1,0:T(8,128)(2,1)} async-done(((bf16[512,2048]{1,0:T(8,128)(2,1)}), bf16[1024,2048]{1,0:T(8,128)(2,1)}) %all-gather.2.cloned.1.call-update) | async-done | bytes 4194320 | tf_op jit(solution)/shard_map/all_gather | solution.py:189
  975.6 183.1 %reduce-scatter.11.cloned.1.call-done = bf16[128,2,2048]{2,0,1:T(8,128)(2,1)} async-done(((bf16[2048,2,2048]{2,0,1:T(8,128)(2,1)}), bf16[128,2,2048]{2,0,1:T(8,128)(2,1)}) %reduce-scatter.11.cloned.1.call-update) | async-done | bytes 1048592 | tf_op jit(solution)/shard_map/reduce_scatter | solution.py:191
  (419 shorter events, 436.5 us)
Async XLA Ops:
  8.0 137.2 %copy-start = (bf16[2048,256]{1,0:T(8,128)(2,1)S(1)}, bf16[2048,256]{1,0:T(8,128)(2,1)}, u32[]{:S(2)}) copy-start(bf16[2048,256]{1,0:T(8,128)(2,1)} %param.21) | copy-start | bytes 3145732
  8.0 658.2 %all-reduce.29.cloned.1.call-start = ((), (), s32[]{:S(2)}) async-start(), calls=%async_computation.4 | async-start | bytes 8388608 | tf_op jit(solution)/shard_map/psum | solution.py:155
  8.8 51.4 %copy-start.79 = (s32[8]{0:T(128)}, s32[8]{0:T(128)S(1)}, u32[]{:S(2)}) copy-start(s32[8]{0:T(128)S(1)} %broadcast_maximum_fusion) | copy-start | bytes 100
  9.5 139.9 %copy-start.76 = (pred[8]{0:T(512)(128)(4,1)}, pred[8]{0:T(512)(128)(4,1)S(1)}, u32[]{:S(2)}) copy-start(pred[8]{0:T(512)(128)(4,1)S(1)} %get-tuple-element.411) | copy-start | bytes 28
  12.6 32.9 %copy-start.58 = (f32[1024]{0:T(1024)}, f32[1024]{0:T(1024)S(1)}, u32[]{:S(2)}) copy-start(f32[1024]{0:T(1024)S(1)} %add_rsqrt_fusion.1) | copy-start | bytes 12292
  12.6 32.8 %copy-start.60 = (f32[5,2048]{1,0:T(8,128)S(1)}, f32[5,2048]{1,0:T(8,128)}, u32[]{:S(2)}) copy-start(f32[5,2048]{1,0:T(8,128)} %param.23) | copy-start | bytes 122884
  12.6 32.9 %copy-start.6 = (bf16[1024,2048]{1,0:T(8,128)(2,1)S(1)}, bf16[1024,2048]{1,0:T(8,128)(2,1)}, u32[]{:S(2)}) copy-start(bf16[1024,2048]{1,0:T(8,128)(2,1)} %param.18) | copy-start | bytes 12582916
  12.6 32.9 %copy-start.48 = (f32[2048]{0:T(1024)S(1)}, f32[2048]{0:T(1024)}, u32[]{:S(2)}) copy-start(f32[2048]{0:T(1024)} %param.19) | copy-start | bytes 24580
  93.9 35.0 %copy-start.51 = (s32[8]{0:T(128)S(1)}, s32[8]{0:T(128)}, u32[]{:S(2)}) copy-start(s32[8]{0:T(128)} %param.31) | copy-start | bytes 100
  128.8 32.9 %copy-start.34 = (f32[8,8]{0,1:T(8,128)}, f32[8,8]{0,1:T(8,128)S(1)}, u32[]{:S(2)}) copy-start(f32[8,8]{0,1:T(8,128)S(1)} %fusion.143) | copy-start | bytes 772
  289.8 37.3 %copy-start.61 = (f32[1024]{0:T(1024)}, f32[1024]{0:T(1024)S(1)}, u32[]{:S(2)}) copy-start(f32[1024]{0:T(1024)S(1)} %add_rsqrt_fusion) | copy-start | bytes 12292
  305.2 441.2 %reduce-scatter.9.cloned.1.call-start = ((), (), s32[]{:S(2)}) async-start(), calls=%async_computation.5 | async-start | bytes 6291456 | tf_op jit(solution)/shard_map/reduce_scatter | solution.py:181
  532.1 40.7 %copy-start.10 = (f32[8,128,32]{2,0,1:T(8,128)S(1)}, f32[8,128,32]{2,0,1:T(8,128)}, u32[]{:S(2)}) copy-start(f32[8,128,32]{2,0,1:T(8,128)} %copy-done.9) | copy-start | bytes 393220
  532.1 43.3 %copy-start.13 = (f32[8,128,32]{2,0,1:T(8,128)S(1)}, f32[8,128,32]{2,0,1:T(8,128)}, u32[]{:S(2)}) copy-start(f32[8,128,32]{2,0,1:T(8,128)} %copy.149) | copy-start | bytes 393220
  690.3 164.1 %reduce-scatter.13.cloned.1.call-start = ((), (), s32[]{:S(2)}) async-start(), calls=%async_computation.9 | async-start | bytes 557056
  694.4 222.4 %reduce-scatter.15.cloned.1.call-start = ((), (), s32[]{:S(2)}) async-start(), calls=%async_computation.10 | async-start | bytes 8912896
  722.2 253.4 %all-gather.2.cloned.1.call-start = ((), (), s32[]{:S(2)}) async-start(), calls=%async_computation.6 | async-start | bytes 6291456 | tf_op jit(solution)/shard_map/all_gather | solution.py:189
  755.8 402.9 %reduce-scatter.11.cloned.1.call-start = ((), (), s32[]{:S(2)}) async-start(), calls=%async_computation.7 | async-start | bytes 17825792 | tf_op jit(solution)/shard_map/reduce_scatter | solution.py:191
  785.4 69.0 %copy-start.81 = (f32[256]{0:T(256)S(1)}, f32[256]{0:T(256)}, u32[]{:S(2)}) copy-start(f32[256]{0:T(256)} %get-tuple-element.326) | copy-start | bytes 3076
  785.4 69.0 %copy-start.82 = (f32[256]{0:T(256)S(1)}, f32[256]{0:T(256)}, u32[]{:S(2)}) copy-start(f32[256]{0:T(256)} %get-tuple-element.327) | copy-start | bytes 3076
  785.4 69.0 %copy-start.83 = (f32[256]{0:T(256)S(1)}, f32[256]{0:T(256)}, u32[]{:S(2)}) copy-start(f32[256]{0:T(256)} %get-tuple-element.328) | copy-start | bytes 3076
  785.4 69.0 %copy-start.84 = (f32[256]{0:T(256)S(1)}, f32[256]{0:T(256)}, u32[]{:S(2)}) copy-start(f32[256]{0:T(256)} %get-tuple-element.329) | copy-start | bytes 3076
  785.4 69.0 %copy-start.85 = (f32[256]{0:T(256)S(1)}, f32[256]{0:T(256)}, u32[]{:S(2)}) copy-start(f32[256]{0:T(256)} %get-tuple-element.330) | copy-start | bytes 3076
  785.4 376.9 %all-reduce.31.cloned.1.call-start = ((), (), s32[]{:S(2)}) async-start(), calls=%async_computation.8 | async-start | bytes 4194304 | tf_op jit(solution)/shard_map/psum | solution.py:204
  (81 other events, 998.9 us)
Sparse Core Ops, SparseCore 0:
  305.3 109.7 all-reduce.28
  690.4 55.9 reduce-scatter.8
  750.5 56.5 reduce-scatter.12
  811.6 105.2 reduce-scatter.14
  918.9 56.6 all-gather.1
  980.1 178.5 reduce-scatter.10
Sparse Core Ops, SparseCore 1:
  792.7 204.7 all-reduce.30
where the time goes:
time: 1190 us; the launch traced here: 1180 us
  matrix products  397 us (33%)
  waiting for transfers between devices  279 us (23%)
  other arithmetic  188 us (16%)
  local copies, waits for them, and re-layouts  181 us (15%)
  blocking collectives  113 us (9%)
  between operations  17.5 us (1%)
    reduce_scatter x1, waiting for transfers between devices, local(): lax.psum_scatter(w_zx_part.astype(jnp.bfloat16), 'dp', scatter_dimension=...  183 us
    dot_general x3, matrix products, ssd_mix(): within = jnp.einsum('bijh,bjhp->bihp', weights, x_blocks, precision=highest)  74.5 us
    dot_general x5, matrix products, over_columns(): lax.dot_general(left, right, (((1,), (1,)), ((), ())), preferred_element_...  65.7 us
    psum x1, blocking collectives, local(): lax.psum((conv_x_part, dt_bias_part, a_log_part, d_skip_part, gate_gain_p...  63.7 us
    all_gather x1, waiting for transfers between devices, local(): lax.all_gather(d_input.astype(jnp.bfloat16), 'tensor', axis=0, tiled=True)  56.4 us
    dot_general x5, matrix products, over_tokens(): lax.dot_general(left, right, (((0,), (0,)), ((), ())), preferred_element_...  45.6 us
    dot_general x3, matrix products, ssd_mix(): jnp.einsum('hba,ahpn->bhpn', paths, local_states, precision=highest)  44.6 us
    unnamed x209, local copies, waits for them, and re-layouts  44.2 us
  transfers between devices with their start and end apart: 7, of which 4 were waited for; matrix products, arithmetic and copies ran while one was open for 38% of the time, Pallas kernels for 0%

commit v1 on v0

--- a/solution.py
+++ b/solution.py
@@ -202,7 +202,7 @@
         (conv_x_part, dt_bias_part, a_log_part, d_skip_part, gate_gain_part), "dp"
     )
     norm_gain_grad, w_bc_grad, conv_bc_grad = lax.psum(
-        (norm_gain_part, w_bc_part, conv_bc_part), ("dp", "tensor")
+        lax.psum((norm_gain_part, w_bc_part, conv_bc_part), "tensor"), "dp"
     )
     return (
         mixed,

time: 1190 us -> 1350 us (1.13)
  waiting for transfers between devices: 279 us -> 471 us
  blocking collectives: 113 us -> 81.1 us
    psum x1 -> x2, waiting for transfers between devices: 0.01 us -> 124 us  [the longest x1 96.7 us: local(): lax.psum(lax.psum((norm_gain_part, w_bc_part, conv_bc_part), 'tensor'), '...]
    unnamed x9 -> x10, waiting for transfers between devices: 22.1 us -> 96.3 us
    psum x2, blocking collectives: 103 us -> 70.3 us  [the longest x1 62.2 us: local(): lax.psum(lax.psum((norm_gain_part, w_bc_part, conv_bc_part), 'tensor'), '...]
  transfers between devices with their start and end apart: 7 -> 8, of which waited for: 4 -> 7; matrix products, arithmetic and copies ran while one was open for 38% -> 33% of each run, Pallas kernels for 0% -> 0%
where the time goes in v1:
time: 1350 us; the launch traced here: 1330 us
  waiting for transfers between devices  471 us (35%)
  matrix products  397 us (29%)
  other arithmetic  188 us (14%)
  local copies, waits for them, and re-layouts  181 us (13%)
  blocking collectives  81.1 us (6%)
  between operations  16.1 us (1%)
    reduce_scatter x1, waiting for transfers between devices, local(): lax.psum_scatter(w_zx_part.astype(jnp.bfloat16), 'dp', scatter_dimension=...  183 us
    psum x1, waiting for transfers between devices, local(): lax.psum(lax.psum((norm_gain_part, w_bc_part, conv_bc_part), 'tensor'), '...  96.7 us
    unnamed x10, waiting for transfers between devices  96.3 us
    dot_general x3, matrix products, ssd_mix(): within = jnp.einsum('bijh,bjhp->bihp', weights, x_blocks, precision=highest)  74.5 us
    dot_general x5, matrix products, over_columns(): lax.dot_general(left, right, (((1,), (1,)), ((), ())), preferred_element_...  65.7 us
    psum x1, blocking collectives, local(): lax.psum(lax.psum((norm_gain_part, w_bc_part, conv_bc_part), 'tensor'), '...  62.2 us
    all_gather x1, waiting for transfers between devices, local(): lax.all_gather(d_input.astype(jnp.bfloat16), 'tensor', axis=0, tiled=True)  56.2 us
    dot_general x5, matrix products, over_tokens(): lax.dot_general(left, right, (((0,), (0,)), ((), ())), preferred_element_...  45.5 us
  transfers between devices with their start and end apart: 8, of which 7 were waited for; matrix products, arithmetic and copies ran while one was open for 33% of the time, Pallas kernels for 0%

profile of v1, /device:TPU:0, one launch (start us, length us, event | category | flops | bytes accessed | tf_op | source)
XLA Modules:
  0.0 1334.9 jit_solution(10548173623647683377)
XLA Ops:
  11.8 32.8 %fusion.165 = (bf16[2048,1,2048]{2,1,0:T(2,128)(2,1)}, bf16[2048,1,2048]{2,1,0:T(2,128)(2,1)}) fusion(bf16[2048,2,2048]{2,1,0:T(2,128)(2,1)} %param.20), kind=kLoop, calls=%fused_computation.254 | loop fusion | bytes 33554432 | tf_op jit(solution)/shard_map/slice | solution.py:121
  63.4 16.3 %multiply_convert_fusion.1 = (bf16[8,128,2048]{2,1,0:T(8,128)(2,1)}, f32[8,128,2048]{2,1,0:T(8,128)}) fusion(f32[8,128,2048]{2,1,0:T(8,128)} %copy-done.7, f32[2048]{0:T(1024)S(1)} %bitcast.305, f32[8,3,2048]{2,1,0:T(4,128)S(1)} %select_select_fusion, f32[2048]{0:T(1024)S(1)} %bitcast.307, f32[2048]{0:T(1024)S(1)} %bitcast.301, f32[2048]{0:T(1024)S(1)} %bitcast.303, ...), kind=kLoop, calls=%fused_computation.101 | loop fusion | flops 33554432 | bytes 21209088 | tf_op jit(solution)/shard_map/convert_element_type | solution.py:94
  104.0 23.3 %fusion.171 = f32[8,128,32]{2,0,1:T(8,128)S(1)} fusion(f32[8,128,32]{2,0,1:T(8,128)S(1)} %copy.143), kind=kOutput, calls=%fused_computation.260 | output fusion | flops 4161536 | bytes 262144 | tf_op jit(solution)/shard_map/jvp(jit(cumsum))/reduce_window_sum | solution.py:53
  210.5 21.9 %fusion.39 = f32[8,128,32,64]{1,3,2,0:T(8,128)} fusion(f32[8,128,32,64]{1,3,2,0:T(8,128)} %copy.158, f32[8,128,32,64]{1,3,2,0:T(8,128)S(1)} %fusion.69, f32[32]{0:T(128)S(1)} %copy-done.90, f32[8,128,32]{1,2,0:T(8,128)S(1)} %copy.148, f32[8,128,32]{1,2,0:T(8,128)S(1)} %bitcast.298, f32[8,128,32]{1,2,0:T(8,128)S(1)} %copy-done.36, ...), kind=kOutput, calls=%fused_computation.62 | convolution fusion | flops 3250585600 | bytes 30294144 | tf_op jit(solution)/shard_map/jvp(bijh,bjhp->bihp)/dot_general | solution.py:60
  232.5 16.2 %copy.215 = f32[8,128,32,64]{3,2,1,0:T(8,128)} copy(f32[8,128,32,64]{1,3,2,0:T(8,128)} %fusion.39) | data formatting | bytes 16777216 | tf_op jit(solution)/shard_map/jvp()/reshape | solution.py:70
  263.5 19.7 %multiply_reduce_fusion.11 = (f32[1024]{0:T(1024)S(1)}, f32[1024,2048]{1,0:T(8,128)}, f32[1024,2048]{1,0:T(8,128)}) fusion(f32[1024,2048]{1,0:T(8,128)} %reshape.284, bf16[1024,2048]{1,0:T(8,128)(2,1)} %copy-done.2, bf16[2048,1,2048]{2,1,0:T(2,128)(2,1)} %get-tuple-element.381), kind=kOutput, calls=%fused_computation.85 | convolution fusion | flops 8604613632 | bytes 37752832 | tf_op jit(solution)/shard_map/dot_general | solution.py:121
  304.5 17.0 %multiply_reduce_fusion.2 = (f32[2048]{0:T(1024)}, f32[1024]{0:T(1024)S(1)}, f32[1024,2048]{1,0:T(8,128)}) fusion(f32[1024,2048]{1,0:T(8,128)} %get-tuple-element.375, f32[1024]{0:T(1024)S(1)} %add_rsqrt_fusion, f32[2048]{0:T(1024)S(1)} %copy-done.73, bf16[1024,2048]{1,0:T(8,128)(2,1)} %param.30, bf16[2048,2048]{1,0:T(8,128)(2,1)} %param.29), kind=kOutput, calls=%fused_computation.70 | convolution fusion | flops 8602514432 | bytes 29384704 | tf_op jit(solution)/shard_map/dot_general | solution.py:88
  326.4 20.5 %multiply_reduce_fusion.3 = (f32[2048]{0:T(1024)}, f32[1024,2048]{1,0:T(8,128)}, bf16[1024,2048]{1,0:T(8,128)(2,1)}) fusion(bf16[1024,2048]{1,0:T(8,128)(2,1)} %bitcast.262, f32[1024,2048]{1,0:T(8,128)} %get-tuple-element.415, f32[1024,2048]{1,0:T(8,128)} %get-tuple-element.375, f32[1024]{0:T(1024)S(1)} %fusion.141, f32[1024,2048]{1,0:T(8,128)} %get-tuple-element.416, ...), kind=kLoop, calls=%fused_computation.71 | loop fusion | flops 41940992 | bytes 50356224 | tf_op jit(solution)/shard_map/transpose(jvp())/reduce_sum | solution.py:69
  390.4 21.3 %fusion.106 = f32[32,8,8]{2,1,0:T(8,128)S(1)} fusion(f32[32,64,128,8]{2,3,1,0:T(8,128)S(1)} %fusion.44, f32[8,32,64,128]{3,2,1,0:T(8,128)S(1)} %bitcast.259), kind=kOutput, calls=%fused_computation.159 | convolution fusion | flops 201326592 | bytes 16785408 | tf_op jit(solution)/shard_map/transpose(jvp(hba,ahpn->bhpn))/dot_general | solution.py:64
  428.9 18.2 %fusion.103 = f32[8,128,128]{2,1,0:T(8,128)S(1)} fusion(f32[8,32,64,128]{3,0,2,1:T(8,128)} %convolution_bitcast_fusion.1, f32[8,128,32]{1,2,0:T(8,128)S(1)} %copy-done.29, bf16[8,128,32,64]{1,0,3,2:T(8,128)(2,1)S(1)} %bitcast.266), kind=kOutput, calls=%fused_computation.156 | convolution fusion | flops 3225419776 | bytes 13238272 | tf_op jit(solution)/shard_map/transpose(jvp(bjh,bjhp,bjn->bhpn))/dot_general | solution.py:62
  447.2 15.7 %fusion.98 = f32[8,128,128]{2,1,0:T(8,128)S(1)} fusion(f32[8,32,64,128]{3,0,2,1:T(8,128)S(1)} %bitcast.257, f32[8,128,32,64]{1,0,3,2:T(8,128)S(1)} %bitcast.252, f32[8,128,32]{1,2,0:T(8,128)S(1)} %copy.148), kind=kOutput, calls=%fused_computation.155 | convolution fusion | flops 3223322624 | bytes 17432576 | tf_op jit(solution)/shard_map/transpose(jvp(bin,bhpn->bihp))/dot_general | solution.py:66
  463.0 28.9 %fusion.28 = (f32[8,128,32]{1,2,0:T(8,128)}, f32[8,128,32]{1,2,0:T(8,128)S(1)}, f32[8,128,32]{1,2,0:T(8,128)}, f32[8,128,128]{2,1,0:T(8,128)S(1)}) fusion(f32[8,128,32]{1,2,0:T(8,128)S(1)} %bitcast.299, f32[8,128,32]{1,2,0:T(8,128)S(1)} %copy-done.37, f32[8,128,128]{2,1,0:T(8,128)S(1)} %copy-done.31, pred[128,128]{1,0:T(8,128)(4,1)S(1)} %copy-done.64, ...), kind=kOutput, calls=%fused_computation.44 | convolution fusion | flops 3283910656 | bytes 14303232 | tf_op jit(solution)/shard_map/transpose(jvp(bijh,bjhp->bihp))/dot_general | solution.py:60
  507.7 23.6 %bitcast_add_fusion = f32[8,128,32,64]{1,3,2,0:T(8,128)} fusion(f32[8,128,32,64]{1,3,2,0:T(8,128)} %fusion.65, f32[8,128,32,64]{1,0,3,2:T(8,128)S(1)} %bitcast.255, f32[32]{0:T(128)S(1)} %copy-done.91, f32[8,128,32]{1,2,0:T(8,128)S(1)} %copy-done.29, f32[8,128,32]{1,2,0:T(8,128)S(1)} %bitcast.300, f32[8,128,32]{1,2,0:T(8,128)S(1)} %copy-done.37, ...), kind=kOutput, calls=%fused_computation.58 | convolution fusion | flops 3250585600 | bytes 34488448 | tf_op jit(solution)/shard_map/transpose(jvp(bijh,bjhp->bihp))/dot_general | solution.py:60
  535.7 36.3 %while.31 = (s32[]{:T(128)}, f32[8,32]{1,0:T(8,128)}, f32[32,8,8]{2,1,0:T(8,128)S(1)}, f32[8,32,8,8]{3,2,1,0:T(8,128)}, s32[8]{0:T(128)}, /*index=5*/f32[8,32]{0...) while((s32[]{:T(128)}, f32[8,32]{1,0:T(8,128)}, f32[32,8,8]{2,1,0:T(8,128)S(1)}, ...), condition=%wide.region_15.16_spmd.clone, body=%wide.region_14.15_spmd.clone.sunk | while | flops 420484 | bytes 210855 | solution.py:39
  589.8 18.6 %multiply_reduce_fusion.6 = (f32[2048]{0:T(1024)}, f32[2048]{0:T(1024)}, f32[2048]{0:T(1024)}, f32[2048]{0:T(1024)}, f32[2048]{0:T(1024)}, /*index=5*/f32[8,128,2048]{2,1,0:T(8,128)S(1)}) fusion(f32[8,128,2048]{2,1,0:T(8,128)} %copy-done.7, f32[8,3,2048]{2,1,0:T(4,128)S(1)} %copy-done.19, f32[8,128,2048]{2,1,0:T(8,128)} %get-tuple-element.379, ...), kind=kLoop, calls=%fused_computation.74 | loop fusion | flops 44029952 | bytes 33792000 | tf_op jit(solution)/shard_map/transpose(jvp())/reduce_sum | solution.py:22
  649.8 15.6 %fusion.87 = f32[1024,2048]{1,0:T(8,128)} fusion(bf16[1024,2048]{1,0:T(8,128)(2,1)S(1)} %copy-done.15, bf16[2048,1,2048]{2,1,0:T(2,128)(2,1)} %get-tuple-element.381), kind=kOutput, calls=%fused_computation.142 | convolution fusion | flops 8589934592 | bytes 20971520 | tf_op jit(solution)/shard_map/dot_general | solution.py:88
  665.4 24.1 %multiply_reduce_fusion.8 = (f32[2048]{0:T(1024)S(1)}, bf16[1024,2048]{1,0:T(8,128)(2,1)}, bf16[1024,2048]{1,0:T(8,128)(2,1)}) fusion(bf16[1024,2048]{1,0:T(8,128)(2,1)} %param.18, f32[1024]{0:T(1024)S(1)} %copy-done.59, bf16[1024,2048]{1,0:T(8,128)(2,1)} %all-reduce.30.cloned.1.call-done, f32[1024,2048]{1,0:T(8,128)} %fusion.138, ...), kind=kOutput, calls=%fused_computation.78 | convolution fusion | flops 8613001216 | bytes 54538240 | tf_op jit(solution)/shard_map/dot_general | solution.py:88
  784.6 26.8 %all-reduce.32.cloned.1.call-done = f32[2048,256]{1,0:T(8,128)} async-done(((f32[2048,256]{1,0:T(8,128)}), f32[2048,256]{1,0:T(8,128)}) %all-reduce.32.cloned.1.call-update) | async-done | bytes 2097168 | tf_op jit(solution)/shard_map/psum | solution.py:205
  811.9 59.8 %reduce-scatter.13.cloned.1.call-done = bf16[128,32]{1,0:T(8,128)(2,1)} async-done(((bf16[2048,32]{1,0:T(8,128)(2,1)}), bf16[128,32]{1,0:T(8,128)(2,1)}) %reduce-scatter.13.cloned.1.call-update) | async-done | bytes 8208
  881.2 62.2 %all-reduce.24 = (f32[2048]{0:T(1024)}, f32[5,2048]{1,0:T(8,128)}, f32[5,256]{1,0:T(8,128)}, f32[32]{0:T(128)}, f32[32]{0:T(128)}, /*index=5*/f32[32]{0:T(128)}, f32[2048]{0:T(1024)}) all-reduce(f32[2048]{0:T(1024)S(1)} %get-tuple-element.362, f32[5,2048]{1,0:T(8,128)S(1)} %pad_add_fusion.3, ...), channel_id=1, replica_groups=mesh['dp'=16,'tensor'=2] {'dp'}, use_global_device_ids=true, to_apply=%region_24.25 | all-reduce | flops 15712 | bytes 125696 | tf_op jit(solution)/shard_map/psum | solution.py:204
  943.4 36.4 %reduce-scatter.15.cloned.1.call-done = bf16[128,2048]{1,0:T(8,128)(2,1)} async-done(((bf16[2048,2048]{1,0:T(8,128)(2,1)}), bf16[128,2048]{1,0:T(8,128)(2,1)}) %reduce-scatter.15.cloned.1.call-update) | async-done | bytes 524304
  982.2 56.2 %all-gather.2.cloned.1.call-done = bf16[1024,2048]{1,0:T(8,128)(2,1)} async-done(((bf16[512,2048]{1,0:T(8,128)(2,1)}), bf16[1024,2048]{1,0:T(8,128)(2,1)}) %all-gather.2.cloned.1.call-update) | async-done | bytes 4194320 | tf_op jit(solution)/shard_map/all_gather | solution.py:189
  1038.4 182.7 %reduce-scatter.11.cloned.1.call-done = bf16[128,2,2048]{2,0,1:T(8,128)(2,1)} async-done(((bf16[2048,2,2048]{2,0,1:T(8,128)(2,1)}), bf16[128,2,2048]{2,0,1:T(8,128)(2,1)}) %reduce-scatter.11.cloned.1.call-update) | async-done | bytes 1048592 | tf_op jit(solution)/shard_map/reduce_scatter | solution.py:191
  1224.7 96.7 %all-reduce.34.cloned.1.call-done = f32[2048,256]{1,0:T(8,128)} async-done(((f32[2048,256]{1,0:T(8,128)}), f32[2048,256]{1,0:T(8,128)}) %all-reduce.34.cloned.1.call-update) | async-done | bytes 2097168 | tf_op jit(solution)/shard_map/psum | solution.py:204
  (422 shorter events, 472.6 us)
Async XLA Ops:
  7.2 137.3 %copy-start = (bf16[2048,256]{1,0:T(8,128)(2,1)S(1)}, bf16[2048,256]{1,0:T(8,128)(2,1)}, u32[]{:S(2)}) copy-start(bf16[2048,256]{1,0:T(8,128)(2,1)} %param.21) | copy-start | bytes 3145732
  7.2 658.2 %all-reduce.30.cloned.1.call-start = ((), (), s32[]{:S(2)}) async-start(), calls=%async_computation.4 | async-start | bytes 8388608 | tf_op jit(solution)/shard_map/psum | solution.py:155
  8.0 51.4 %copy-start.79 = (s32[8]{0:T(128)}, s32[8]{0:T(128)S(1)}, u32[]{:S(2)}) copy-start(s32[8]{0:T(128)S(1)} %broadcast_maximum_fusion) | copy-start | bytes 100
  8.6 140.0 %copy-start.76 = (pred[8]{0:T(512)(128)(4,1)}, pred[8]{0:T(512)(128)(4,1)S(1)}, u32[]{:S(2)}) copy-start(pred[8]{0:T(512)(128)(4,1)S(1)} %get-tuple-element.413) | copy-start | bytes 28
  11.7 32.9 %copy-start.58 = (f32[1024]{0:T(1024)}, f32[1024]{0:T(1024)S(1)}, u32[]{:S(2)}) copy-start(f32[1024]{0:T(1024)S(1)} %add_rsqrt_fusion.1) | copy-start | bytes 12292
  11.7 32.8 %copy-start.60 = (f32[5,2048]{1,0:T(8,128)S(1)}, f32[5,2048]{1,0:T(8,128)}, u32[]{:S(2)}) copy-start(f32[5,2048]{1,0:T(8,128)} %param.23) | copy-start | bytes 122884
  11.8 32.9 %copy-start.6 = (bf16[1024,2048]{1,0:T(8,128)(2,1)S(1)}, bf16[1024,2048]{1,0:T(8,128)(2,1)}, u32[]{:S(2)}) copy-start(bf16[1024,2048]{1,0:T(8,128)(2,1)} %param.18) | copy-start | bytes 12582916
  11.8 32.9 %copy-start.48 = (f32[2048]{0:T(1024)S(1)}, f32[2048]{0:T(1024)}, u32[]{:S(2)}) copy-start(f32[2048]{0:T(1024)} %param.19) | copy-start | bytes 24580
  93.1 35.0 %copy-start.51 = (s32[8]{0:T(128)S(1)}, s32[8]{0:T(128)}, u32[]{:S(2)}) copy-start(s32[8]{0:T(128)} %param.31) | copy-start | bytes 100
  128.0 33.0 %copy-start.34 = (f32[8,8]{0,1:T(8,128)}, f32[8,8]{0,1:T(8,128)S(1)}, u32[]{:S(2)}) copy-start(f32[8,8]{0,1:T(8,128)S(1)} %fusion.143) | copy-start | bytes 772
  289.1 37.3 %copy-start.61 = (f32[1024]{0:T(1024)}, f32[1024]{0:T(1024)S(1)}, u32[]{:S(2)}) copy-start(f32[1024]{0:T(1024)S(1)} %add_rsqrt_fusion) | copy-start | bytes 12292
  304.4 441.2 %reduce-scatter.9.cloned.1.call-start = ((), (), s32[]{:S(2)}) async-start(), calls=%async_computation.5 | async-start | bytes 6291456 | tf_op jit(solution)/shard_map/reduce_scatter | solution.py:181
  463.0 30.0 %copy-start.12 = (f32[1024,256]{1,0:T(8,128)S(1)}, f32[1024,256]{1,0:T(8,128)}, u32[]{:S(2)}) copy-start(f32[1024,256]{1,0:T(8,128)} %copy-done.11) | copy-start | bytes 3145732
  463.0 30.0 %copy-start.17 = (f32[8,128,256]{2,1,0:T(8,128)S(1)}, f32[8,128,256]{2,1,0:T(8,128)}, u32[]{:S(2)}) copy-start(f32[8,128,256]{2,1,0:T(8,128)} %get-tuple-element.377) | copy-start | bytes 3145732
  463.0 30.0 %copy-start.33 = (f32[8,3,256]{2,1,0:T(4,128)S(1)}, f32[8,3,256]{2,1,0:T(4,128)}, u32[]{:S(2)}) copy-start(f32[8,3,256]{2,1,0:T(4,128)} %copy-done.32) | copy-start | bytes 73732
  531.3 40.7 %copy-start.10 = (f32[8,128,32]{2,0,1:T(8,128)S(1)}, f32[8,128,32]{2,0,1:T(8,128)}, u32[]{:S(2)}) copy-start(f32[8,128,32]{2,0,1:T(8,128)} %copy-done.9) | copy-start | bytes 393220
  531.3 43.3 %copy-start.13 = (f32[8,128,32]{2,0,1:T(8,128)S(1)}, f32[8,128,32]{2,0,1:T(8,128)}, u32[]{:S(2)}) copy-start(f32[8,128,32]{2,0,1:T(8,128)} %copy.149) | copy-start | bytes 393220
  689.5 121.9 %all-reduce.32.cloned.1.call-start = ((), (), s32[]{:S(2)}) async-start(), calls=%async_computation.8 | async-start | bytes 4194304 | tf_op jit(solution)/shard_map/psum | solution.py:205
  694.4 177.2 %reduce-scatter.13.cloned.1.call-start = ((), (), s32[]{:S(2)}) async-start(), calls=%async_computation.10 | async-start | bytes 557056
  698.5 281.3 %reduce-scatter.15.cloned.1.call-start = ((), (), s32[]{:S(2)}) async-start(), calls=%async_computation.11 | async-start | bytes 8912896
  726.2 312.1 %all-gather.2.cloned.1.call-start = ((), (), s32[]{:S(2)}) async-start(), calls=%async_computation.6 | async-start | bytes 6291456 | tf_op jit(solution)/shard_map/all_gather | solution.py:189
  755.0 466.0 %reduce-scatter.11.cloned.1.call-start = ((), (), s32[]{:S(2)}) async-start(), calls=%async_computation.7 | async-start | bytes 17825792 | tf_op jit(solution)/shard_map/reduce_scatter | solution.py:191
  784.6 96.6 %copy-start.75 = (f32[2048]{0:T(1024)S(1)}, f32[2048]{0:T(1024)}, u32[]{:S(2)}) copy-start(f32[2048]{0:T(1024)} %get-tuple-element.319) | copy-start | bytes 24580
  784.6 536.8 %all-reduce.34.cloned.1.call-start = ((), (), s32[]{:S(2)}) async-start(), calls=%async_computation.9 | async-start | bytes 4194304 | tf_op jit(solution)/shard_map/psum | solution.py:204
  (82 other events, 1199.0 us)
Sparse Core Ops, SparseCore 0:
  304.5 109.7 all-reduce.29
  689.6 55.9 reduce-scatter.8
  748.5 62.9 all-reduce.31
  815.9 55.7 reduce-scatter.12
  875.5 104.2 reduce-scatter.14
  981.8 56.5 all-gather.1
  1042.5 178.5 reduce-scatter.10
  1224.6 96.7 all-reduce.33
